TPU v7x, 32 devices: a whole 2x2x4 slice. The times are simulated.
32 devices in a mesh: ctx: 8 (over z, x), head: 4 (over y, core).
Axes of the slice: x: 2, y: 2, z: 4, core: 2. Of those that a mesh axis runs over, the one named last changes fastest.
Arguments:
- query_rows: bfloat16 [1536, 4096], P('ctx', 'head'), may hold values from -4.5 to 4.5
- key_rows: bfloat16 [1536, 512], P('ctx'), may hold values from -4.5 to 4.5
- value_rows: bfloat16 [1536, 512], P('ctx'), may hold values from -6 to 6
- w_out: bfloat16 [4096, 2048], P('head'), may hold values from -0.09375 to 0.09375
Outputs:
- mixed: bfloat16 [1536, 2048], P('ctx', 'head')
All inputs are finite; a program needn't handle non-finite values.
Results may differ from a plain program's by a relative error of at most 0.019.
Values may be sent and summed in bfloat16 or wider, within the bound.
No kernel may reach another device: no remote copies, remote signals or barrier semaphores. Data moves between devices by JAX's collectives and lax.ppermute only.
A program may use at most 64 MiB of HBM per device.

v0:
```python
import math
import jax
import jax.numpy as jnp
from jax import lax
from jax.sharding import PartitionSpec as P

KVH = 4
HD = 128
negative = -1e30


def attend(state, queries_half, position_half, block_keys, block_values, key_start, score_scale):
    maximum, denominator, numerator = state
    key_count = block_keys.shape[0]
    scores = (
        jnp.einsum("thd,kd->thk", queries_half, block_keys, preferred_element_type=jnp.float32)
        * score_scale
    )
    key_positions = key_start + jnp.arange(key_count, dtype=jnp.int32)
    allowed = key_positions[None, None, :] <= position_half[:, None, None]
    scores = jnp.where(allowed, scores, negative)
    updated = jnp.maximum(maximum, jnp.max(scores, axis=2))
    weights = jnp.where(allowed, jnp.exp(scores - updated[:, :, None]), 0.0)
    factor = jnp.exp(maximum - updated)
    denominator = denominator * factor + jnp.sum(weights, axis=2)
    numerator = numerator * factor[:, :, None] + jnp.einsum(
        "thk,kd->thd",
        weights.astype(jnp.bfloat16),
        block_values,
        preferred_element_type=jnp.float32,
    )
    return (updated, denominator, numerator)


def on_device(query_rows, key_rows, value_rows, w_out):
    local_tokens = query_rows.shape[0]
    head_count = lax.axis_size("head")
    local_heads = query_rows.shape[1] // HD
    kv_head = lax.axis_index("head") * KVH // head_count
    own_keys = lax.dynamic_slice_in_dim(key_rows, kv_head * HD, HD, 1)
    own_values = lax.dynamic_slice_in_dim(value_rows, kv_head * HD, HD, 1)
    row_numbers = jnp.arange(local_tokens, dtype=jnp.int32)
    positions = lax.axis_index("ctx") * local_tokens + row_numbers
    heads_view = query_rows.reshape(local_tokens, local_heads, HD)
    half_rows = local_tokens // 2
    halves = [
        (heads_view[:half_rows], positions[:half_rows]),
        (heads_view[half_rows:], positions[half_rows:]),
    ]
    score_scale = 1.0 / math.sqrt(HD)
    initial = (
        jnp.full((half_rows, local_heads), negative, jnp.float32),
        jnp.zeros((half_rows, local_heads), jnp.float32),
        jnp.zeros((half_rows, local_heads, HD), jnp.float32),
    )
    piece_keys = lax.all_gather(own_keys, "ctx", axis=0, tiled=True)
    piece_values = lax.all_gather(own_values, "ctx", axis=0, tiled=True)
    piece_rows = piece_keys.shape[0]
    block_rows = math.gcd(piece_rows, local_tokens * max(1, 1024 // local_tokens))
    block_total = piece_rows // block_rows

    def one_block(block_number, states):
        block_start = block_number * block_rows
        block_keys = lax.dynamic_slice_in_dim(piece_keys, block_start, block_rows, 0)
        block_values = lax.dynamic_slice_in_dim(piece_values, block_start, block_rows, 0)
        results = []
        for (queries_half, position_half), state in zip(halves, states):
            state = attend(
                state,
                queries_half,
                position_half,
                block_keys,
                block_values,
                block_start,
                score_scale,
            )
            results.append(state)
        return tuple(results)

    states = lax.fori_loop(0, block_total, one_block, (initial, initial))
    pieces = [state[2] / state[1][:, :, None] for state in states]
    attended = (
        jnp.concatenate(pieces, axis=0).astype(jnp.bfloat16).reshape(local_tokens, local_heads * HD)
    )
    partial_sums = jnp.dot(attended, w_out, preferred_element_type=jnp.float32)
    return lax.psum_scatter(
        partial_sums.astype(jnp.bfloat16), "head", scatter_dimension=1, tiled=True
    )


def solution(mesh):
    placed = (P("ctx", "head"), P("ctx", None), P("ctx", None), P("head", None))
    return jax.shard_map(
        on_device, mesh=mesh, in_specs=placed, out_specs=P("ctx", "head"), check_vma=False
    )
```

profile of v0, /device:TPU:0, one launch (start us, length us, event | category | flops | bytes accessed | tf_op | source)
XLA Modules:
  0.0 131.6 jit_solution(6765854102075202055)
XLA Ops:
  6.7 0.8 copy-done
  7.5 0.8 constant_dynamic-slice_fusion
  8.3 32.9 %all_gather.7 = bf16[1536,128]{1,0:T(8,128)(2,1)S(1)} all-gather(bf16[192,128]{1,0:T(8,128)(2,1)S(1)} %constant_dynamic-slice_fusion), channel_id=1, replica_groups=mesh['ctx'=8,'head'=4] {'ctx'}, dimensions={0}, use_global_device_ids=true | all-gather | bytes 442368 | tf_op jit(solution)/shard_map/all_gather | solution.py:57
  41.2 30.9 %all_gather.6 = bf16[1536,128]{1,0:T(8,128)(2,1)S(1)} all-gather(bf16[192,128]{1,0:T(8,128)(2,1)S(1)} %constant_dynamic-slice_fusion.1), channel_id=1, replica_groups=mesh['ctx'=8,'head'=4] {'ctx'}, dimensions={0}, use_global_device_ids=true | all-gather | bytes 442368 | tf_op jit(solution)/shard_map/all_gather | solution.py:56
  72.1 1.0 slice_bitcast_fusion
  73.3 22.4 %while.24 = (s32[]{:T(128)}, f32[96,8]{0,1:T(8,128)S(1)}, f32[96,8]{0,1:T(8,128)S(1)}, f32[96,8,128]{2,1,0:T(8,128)S(1)}, f32[96,8]{0,1:T(8,128)S(1)}, /*index=5...) while((s32[]{:T(128)}, f32[96,8]{0,1:T(8,128)S(1)}, ...), condition=%wide.region_5.6_spmd.clone, body=%wide.region_0.5_spmd.clone.sunk | while | flops 153693888 | bytes 7399925 | solution.py:80
  73.4 0.3 fusion.51
  74.0 0.3 copy.33
  74.3 0.3 fusion.52
  74.6 0.2 fusion.53
  75.0 0.3 convolution_add_fusion.4
  75.4 0.3 copy.35
  75.7 0.3 convolution_add_fusion.5
  76.2 0.3 fusion.51
  76.8 0.3 copy.33
  77.1 0.3 fusion.52
  77.5 0.2 fusion.53
  77.8 0.3 convolution_add_fusion.4
  78.2 0.3 copy.35
  78.6 0.3 convolution_add_fusion.5
  79.0 0.3 fusion.51
  79.6 0.3 copy.33
  79.9 0.3 fusion.52
  80.2 0.2 fusion.53
  80.6 0.3 convolution_add_fusion.4
  81.0 0.3 copy.35
  81.3 0.3 convolution_add_fusion.5
  81.8 0.3 fusion.51
  82.4 0.3 copy.33
  82.7 0.3 fusion.52
  83.1 0.2 fusion.53
  83.4 0.3 convolution_add_fusion.4
  83.8 0.3 copy.35
  84.2 0.3 convolution_add_fusion.5
  84.6 0.3 fusion.51
  85.2 0.3 copy.33
  85.5 0.3 fusion.52
  85.8 0.2 fusion.53
  86.2 0.3 convolution_add_fusion.4
  86.6 0.3 copy.35
  86.9 0.3 convolution_add_fusion.5
  87.4 0.3 fusion.51
  88.0 0.3 copy.33
  88.3 0.3 fusion.52
  88.7 0.2 fusion.53
  89.0 0.3 convolution_add_fusion.4
  89.4 0.3 copy.35
  89.8 0.3 convolution_add_fusion.5
  90.2 0.3 fusion.51
  90.8 0.3 copy.33
  91.1 0.3 fusion.52
  91.4 0.2 fusion.53
  91.8 0.3 convolution_add_fusion.4
  92.2 0.3 copy.35
  92.5 0.3 convolution_add_fusion.5
  93.0 0.3 fusion.51
  93.6 0.3 copy.33
  93.9 0.3 fusion.52
  94.3 0.2 fusion.53
  94.6 0.3 convolution_add_fusion.4
  95.0 0.3 copy.35
  95.4 0.3 convolution_add_fusion.5
  96.3 4.1 %convolution_convert_fusion = bf16[192,2048]{1,0:T(8,128)(2,1)} fusion(bf16[1024,2048]{1,0:T(8,128)(2,1)} %param.9, bf16[96,1024]{1,0:T(8,128)(2,1)S(1)} %bitcast.61, bf16[96,1024]{1,0:T(8,128)(2,1)S(1)} %bitcast.62), kind=kOutput, calls=%fused_computation.39 | convolution fusion | flops 806486016 | bytes 5373952 | tf_op jit(solution)/shard_map/dot_general | solution.py:85
  100.4 24.3 %reduce-scatter.2.cloned.1.call-done = bf16[192,512]{1,0:T(8,128)(2,1)} async-done(((bf16[192,2048]{1,0:T(8,128)(2,1)}), bf16[192,512]{1,0:T(8,128)(2,1)}) %reduce-scatter.2.cloned.1.call-update) | async-done | bytes 196624 | tf_op jit(solution)/shard_map/reduce_scatter | solution.py:86
  (99 shorter events, 4.9 us)
Async XLA Ops:
  6.5 0.9 copy-start
  6.5 118.2 %reduce-scatter.2.cloned.1.call-start = ((), (), s32[]{:S(2)}) async-start(), calls=%async_computation.1 | async-start | bytes 983040 | tf_op jit(solution)/shard_map/reduce_scatter | solution.py:86
Sparse Core Ops, SparseCore 0:
  100.5 24.1 reduce-scatter.1
where the time goes:
time: 132 us
  blocking collectives  63.9 us (48%)
  waiting for transfers between devices  24.4 us (18%)
  matrix products  14.4 us (11%)
  between operations  13.5 us (10%)
  local copies, waits for them, and re-layouts  9.8 us (7%)
  other arithmetic  4.6 us (3%)
    all_gather x1, blocking collectives, on_device(): piece_values = lax.all_gather(own_values, 'ctx', axis=0, tiled=True)  32.9 us
    all_gather x1, blocking collectives, on_device(): piece_keys = lax.all_gather(own_keys, 'ctx', axis=0, tiled=True)  30.9 us
    reduce_scatter x1, waiting for transfers between devices, on_device(): lax.psum_scatter(partial_sums.astype(jnp.bfloat16), 'head', scatter_dimen...  24.3 us
    convert_element_type x16, local copies, waits for them, and re-layouts, attend(): weights.astype(jnp.bfloat16)  5.23 us
    dot_general x16, matrix products, attend(): jnp.einsum('thd,kd->thk', queries_half, block_keys, preferred_element_typ...  5.2 us
    dot_general x16, matrix products, attend(): jnp.einsum('thk,kd->thd', weights.astype(jnp.bfloat16), block_values, pre...  5.12 us
    dot_general x1, matrix products, on_device(): partial_sums = jnp.dot(attended, w_out, preferred_element_type=jnp.float32)  4.08 us
    convert_element_type x16, other arithmetic, attend(): weights.astype(jnp.bfloat16)  3.24 us
  transfers between devices with their start and end apart: 1, of which 1 were waited for; matrix products, arithmetic and copies ran while one was open for 0% of the time, Pallas kernels for 0%

commit v1 on v0

--- a/solution.py
+++ b/solution.py
@@ -7,6 +7,12 @@
 KVH = 4
 HD = 128
 negative = -1e30
+
+
+def joined_along(pieces, dim):
+    pieces = jnp.moveaxis(pieces, 0, dim)
+    shape = pieces.shape
+    return pieces.reshape(*shape[:dim], shape[dim] * shape[dim + 1], *shape[dim + 2 :])
 
 
 def attend(state, queries_half, position_half, block_keys, block_values, key_start, score_scale):
@@ -54,7 +60,19 @@
         jnp.zeros((half_rows, local_heads, HD), jnp.float32),
     )
     piece_keys = lax.all_gather(own_keys, "ctx", axis=0, tiled=True)
-    piece_values = lax.all_gather(own_values, "ctx", axis=0, tiled=True)
+    size = lax.axis_size("ctx")
+    pairs = [(i, (i + 1) % size) for i in range(size)]
+    back = [(b, a) for a, b in pairs]
+    lower, upper = ([], [])
+    for step in range(size - 1):
+        if step % 2 == 0:
+            lower.append(lax.ppermute(lower[-1] if lower else own_values, "ctx", pairs))
+        else:
+            upper.append(lax.ppermute(upper[-1] if upper else own_values, "ctx", back))
+    blocks = jnp.stack([*lower[::-1], own_values, *upper])
+    shift = lax.axis_index("ctx") - len(lower)
+    blocks = blocks[(jnp.arange(size) - shift) % size]
+    piece_values = joined_along(blocks, 0)
     piece_rows = piece_keys.shape[0]
     block_rows = math.gcd(piece_rows, local_tokens * max(1, 1024 // local_tokens))
     block_total = piece_rows // block_rows

time: 132 us -> 125 us (0.947)
  blocking collectives: 63.9 us -> 31.4 us
  starting transfers between devices: 0.01 us -> 15.5 us
  waiting for transfers between devices: 24.4 us -> 33.5 us
    all_gather x1 -> x0, blocking collectives: 32.9 us -> none  [on_device(): piece_values = lax.all_gather(own_values, 'ctx', axis=0, tiled=True)]
    ppermute x0 -> x7, starting transfers between devices: none -> 15.5 us  [the longest x3 13.6 us: on_device(): upper.append(lax.ppermute(upper[-1] if upper else own_values, 'ctx', back))]
    ppermute x0 -> x7, waiting for transfers between devices: none -> 9.5 us  [the longest x4 9.49 us: on_device(): lower.append(lax.ppermute(lower[-1] if lower else own_values, 'ctx', pairs))]
  transfers between devices with their start and end apart: 1 -> 8, of which waited for: 1 -> 4; matrix products, arithmetic and copies ran while one was open for 0% -> 2% of each run, Pallas kernels for 0% -> 0%
where the time goes in v1:
time: 125 us
  waiting for transfers between devices  33.5 us (27%)
  blocking collectives  31.4 us (25%)
  starting transfers between devices  15.5 us (12%)
  matrix products  14.4 us (12%)
  between operations  13.6 us (11%)
  local copies, waits for them, and re-layouts  10.6 us (8%)
  other arithmetic  4.63 us (4%)
    all_gather x1, blocking collectives, on_device(): piece_keys = lax.all_gather(own_keys, 'ctx', axis=0, tiled=True)  31.4 us
    reduce_scatter x1, waiting for transfers between devices, on_device(): lax.psum_scatter(partial_sums.astype(jnp.bfloat16), 'head', scatter_dimen...  24 us
    ppermute x3, starting transfers between devices, on_device(): upper.append(lax.ppermute(upper[-1] if upper else own_values, 'ctx', back))  13.6 us
    ppermute x4, waiting for transfers between devices, on_device(): lower.append(lax.ppermute(lower[-1] if lower else own_values, 'ctx', pairs))  9.49 us
    convert_element_type x16, local copies, waits for them, and re-layouts, attend(): weights.astype(jnp.bfloat16)  5.27 us
    dot_general x16, matrix products, attend(): jnp.einsum('thd,kd->thk', queries_half, block_keys, preferred_element_typ...  5.2 us
    dot_general x16, matrix products, attend(): jnp.einsum('thk,kd->thd', weights.astype(jnp.bfloat16), block_values, pre...  5.15 us
    dot_general x1, matrix products, on_device(): partial_sums = jnp.dot(attended, w_out, preferred_element_type=jnp.float32)  4.09 us
  transfers between devices with their start and end apart: 8, of which 4 were waited for; matrix products, arithmetic and copies ran while one was open for 2% of the time, Pallas kernels for 0%

profile of v1, /device:TPU:0, one launch (start us, length us, event | category | flops | bytes accessed | tf_op | source)
XLA Modules:
  0.0 124.7 jit_solution(14989432439113545639)
XLA Ops:
  6.5 0.8 constant_dynamic-slice_fusion
  7.4 6.0 %collective-permute-start.4 = (bf16[192,128]{1,0:T(8,128)(2,1)S(1)}, bf16[192,128]{1,0:T(8,128)(2,1)S(1)}, u32[]{:S(2)}, u32[]{:S(2)}) collective-permute-start(bf16[192,128]{1,0:T(8,128)(2,1)S(1)} %constant_dynamic-slice_fusion), channel_id=1, source_target_pairs={{4,0},{8,4},{12,8},{16,12},{20,16},{24,20},{28,24},{0,28},{5,1},{9... | collective-permute-start | bytes 147464 | tf_op jit(solution)/shard_map/ppermute | solution.py:71
  13.5 1.0 slice_bitcast_fusion
  14.6 5.5 %collective-permute-done = bf16[192,128]{1,0:T(8,128)(2,1)S(1)} collective-permute-done((bf16[192,128]{1,0:T(8,128)(2,1)S(1)}, bf16[192,128]{1,0:T(8,128)(2,1)S(1)}, u32[]{:S(2)}, u32[]{:S(2)}) %collective-permute-start) | collective-permute-done | bytes 49184 | tf_op jit(solution)/shard_map/ppermute | solution.py:69
  20.2 31.4 %all_gather.3 = bf16[1536,128]{1,0:T(8,128)(2,1)S(1)} all-gather(bf16[192,128]{1,0:T(8,128)(2,1)S(1)} %constant_dynamic-slice_fusion.1), channel_id=1, replica_groups=mesh['ctx'=8,'head'=4] {'ctx'}, dimensions={0}, use_global_device_ids=true | all-gather | bytes 442368 | tf_op jit(solution)/shard_map/all_gather | solution.py:62
  51.6 1.9 %collective-permute-start.2 = (bf16[192,128]{1,0:T(8,128)(2,1)S(1)}, bf16[192,128]{1,0:T(8,128)(2,1)S(1)}, u32[]{:S(2)}, u32[]{:S(2)}) collective-permute-start(bf16[192,128]{1,0:T(8,128)(2,1)S(1)} %collective-permute-done.1), channel_id=1, source_target_pairs={{0,4},{4,8},{8,12},{12,16},{16,20},{20,24},{24,28},{28,0},{1,5},{5... | collective-permute-start | bytes 147464 | tf_op jit(solution)/shard_map/ppermute | solution.py:69
  53.5 2.8 %collective-permute-start.5 = (bf16[192,128]{1,0:T(8,128)(2,1)S(1)}, bf16[192,128]{1,0:T(8,128)(2,1)S(1)}, u32[]{:S(2)}, u32[]{:S(2)}) collective-permute-start(bf16[192,128]{1,0:T(8,128)(2,1)S(1)} %collective-permute-done.4), channel_id=1, source_target_pairs={{4,0},{8,4},{12,8},{16,12},{20,16},{24,20},{28,24},{0,28},{5,1},{9... | collective-permute-start | bytes 147464 | tf_op jit(solution)/shard_map/ppermute | solution.py:71
  56.4 2.0 %collective-permute-done.2 = bf16[192,128]{1,0:T(8,128)(2,1)S(1)} collective-permute-done((bf16[192,128]{1,0:T(8,128)(2,1)S(1)}, bf16[192,128]{1,0:T(8,128)(2,1)S(1)}, u32[]{:S(2)}, u32[]{:S(2)}) %collective-permute-start.2) | collective-permute-done | bytes 49184 | tf_op jit(solution)/shard_map/ppermute | solution.py:69
  58.4 4.7 %collective-permute-start.6 = (bf16[192,128]{1,0:T(8,128)(2,1)S(1)}, bf16[192,128]{1,0:T(8,128)(2,1)S(1)}, u32[]{:S(2)}, u32[]{:S(2)}) collective-permute-start(bf16[192,128]{1,0:T(8,128)(2,1)S(1)} %collective-permute-done.5), channel_id=1, source_target_pairs={{4,0},{8,4},{12,8},{16,12},{20,16},{24,20},{28,24},{0,28},{5,1},{9... | collective-permute-start | bytes 147464 | tf_op jit(solution)/shard_map/ppermute | solution.py:71
  63.2 2.0 %collective-permute-done.3 = bf16[192,128]{1,0:T(8,128)(2,1)S(1)} collective-permute-done((bf16[192,128]{1,0:T(8,128)(2,1)S(1)}, bf16[192,128]{1,0:T(8,128)(2,1)S(1)}, u32[]{:S(2)}, u32[]{:S(2)}) %collective-permute-start.3) | collective-permute-done | bytes 49184 | tf_op jit(solution)/shard_map/ppermute | solution.py:69
  65.2 0.8 bitcast_dynamic-update-slice_fusion.3
  66.1 0.6 gather_fusion
  66.7 22.4 %while.24 = (s32[]{:T(128)}, f32[96,8]{0,1:T(8,128)S(1)}, f32[96,8]{0,1:T(8,128)S(1)}, f32[96,8,128]{2,1,0:T(8,128)S(1)}, f32[96,8]{0,1:T(8,128)S(1)}, /*index=5...) while((s32[]{:T(128)}, f32[96,8]{0,1:T(8,128)S(1)}, ...), condition=%wide.region_5.6_spmd.clone, body=%wide.region_0.5_spmd.clone.sunk | while | flops 153693888 | bytes 7399925 | solution.py:98
  66.8 0.3 fusion.53
  67.4 0.3 copy.33
  67.7 0.3 fusion.54
  68.1 0.2 fusion.55
  68.4 0.3 convolution_add_fusion.4
  68.8 0.3 copy.35
  69.2 0.3 convolution_add_fusion.5
  69.6 0.3 fusion.53
  70.2 0.3 copy.33
  70.5 0.3 fusion.54
  71.2 0.3 convolution_add_fusion.4
  71.6 0.3 copy.35
  72.0 0.3 convolution_add_fusion.5
  72.4 0.3 fusion.53
  73.0 0.3 copy.33
  73.3 0.3 fusion.54
  74.0 0.3 convolution_add_fusion.4
  74.4 0.3 copy.35
  74.8 0.3 convolution_add_fusion.5
  75.2 0.3 fusion.53
  75.8 0.3 copy.33
  76.1 0.3 fusion.54
  76.8 0.3 convolution_add_fusion.4
  77.2 0.3 copy.35
  77.6 0.3 convolution_add_fusion.5
  78.0 0.3 fusion.53
  78.6 0.3 copy.33
  78.9 0.3 fusion.54
  79.6 0.3 convolution_add_fusion.4
  80.0 0.3 copy.35
  80.4 0.3 convolution_add_fusion.5
  80.8 0.3 fusion.53
  81.4 0.3 copy.33
  81.7 0.3 fusion.54
  82.4 0.3 convolution_add_fusion.4
  82.8 0.3 copy.35
  83.2 0.3 convolution_add_fusion.5
  83.6 0.3 fusion.53
  84.2 0.3 copy.33
  84.5 0.3 fusion.54
  85.2 0.3 convolution_add_fusion.4
  85.6 0.3 copy.35
  86.0 0.3 convolution_add_fusion.5
  86.5 0.3 fusion.53
  87.0 0.3 copy.33
  87.3 0.3 fusion.54
  88.0 0.3 convolution_add_fusion.4
  88.5 0.3 copy.35
  88.8 0.3 convolution_add_fusion.5
  89.7 4.1 %convolution_convert_fusion = bf16[192,2048]{1,0:T(8,128)(2,1)} fusion(bf16[1024,2048]{1,0:T(8,128)(2,1)} %param.9, bf16[96,1024]{1,0:T(8,128)(2,1)S(1)} %bitcast.81, bf16[96,1024]{1,0:T(8,128)(2,1)S(1)} %bitcast.82), kind=kOutput, calls=%fused_computation.40 | convolution fusion | flops 806486016 | bytes 5373952 | tf_op jit(solution)/shard_map/dot_general | solution.py:103
  93.9 24.0 %reduce-scatter.2.cloned.1.call-done = bf16[192,512]{1,0:T(8,128)(2,1)} async-done(((bf16[192,2048]{1,0:T(8,128)(2,1)}), bf16[192,512]{1,0:T(8,128)(2,1)}) %reduce-scatter.2.cloned.1.call-update) | async-done | bytes 196624 | tf_op jit(solution)/shard_map/reduce_scatter | solution.py:104
  (123 shorter events, 6.5 us)
Async XLA Ops:
  6.5 8.1 %copy-start = (bf16[192,512]{1,0:T(8,128)(2,1)S(1)}, bf16[192,512]{1,0:T(8,128)(2,1)}, u32[]{:S(2)}) copy-start(bf16[192,512]{1,0:T(8,128)(2,1)} %param.7) | copy-start | bytes 589828
  6.5 111.3 %reduce-scatter.2.cloned.1.call-start = ((), (), s32[]{:S(2)}) async-start(), calls=%async_computation.1 | async-start | bytes 983040 | tf_op jit(solution)/shard_map/reduce_scatter | solution.py:104
  7.4 46.1 %collective-permute-start.4 = (bf16[192,128]{1,0:T(8,128)(2,1)S(1)}, bf16[192,128]{1,0:T(8,128)(2,1)S(1)}, u32[]{:S(2)}, u32[]{:S(2)}) collective-permute-start(bf16[192,128]{1,0:T(8,128)(2,1)S(1)} %constant_dynamic-slice_fusion), channel_id=1, source_target_pairs={{4,0},{8,4},{12,8},{16,12},{20,16},{24,20},{28,24},{0,28},{5,1},{9... | collective-permute-start | bytes 147464 | tf_op jit(solution)/shard_map/ppermute | solution.py:71
  13.4 6.8 %collective-permute-start = (bf16[192,128]{1,0:T(8,128)(2,1)S(1)}, bf16[192,128]{1,0:T(8,128)(2,1)S(1)}, u32[]{:S(2)}, u32[]{:S(2)}) collective-permute-start(bf16[192,128]{1,0:T(8,128)(2,1)S(1)} %constant_dynamic-slice_fusion), channel_id=1, source_target_pairs={{0,4},{4,8},{8,12},{12,16},{16,20},{20,24},{24,28},{28,0},{1,5},{5... | collective-permute-start | bytes 147464 | tf_op jit(solution)/shard_map/ppermute | solution.py:69
  20.2 31.4 %collective-permute-start.1 = (bf16[192,128]{1,0:T(8,128)(2,1)S(1)}, bf16[192,128]{1,0:T(8,128)(2,1)S(1)}, u32[]{:S(2)}, u32[]{:S(2)}) collective-permute-start(bf16[192,128]{1,0:T(8,128)(2,1)S(1)} %collective-permute-done), channel_id=1, source_target_pairs={{0,4},{4,8},{8,12},{12,16},{16,20},{20,24},{24,28},{28,0},{1,5},{5... | collective-permute-start | bytes 147464 | tf_op jit(solution)/shard_map/ppermute | solution.py:69
  51.6 6.8 %collective-permute-start.2 = (bf16[192,128]{1,0:T(8,128)(2,1)S(1)}, bf16[192,128]{1,0:T(8,128)(2,1)S(1)}, u32[]{:S(2)}, u32[]{:S(2)}) collective-permute-start(bf16[192,128]{1,0:T(8,128)(2,1)S(1)} %collective-permute-done.1), channel_id=1, source_target_pairs={{0,4},{4,8},{8,12},{12,16},{16,20},{20,24},{24,28},{28,0},{1,5},{5... | collective-permute-start | bytes 147464 | tf_op jit(solution)/shard_map/ppermute | solution.py:69
  53.5 4.9 %collective-permute-start.5 = (bf16[192,128]{1,0:T(8,128)(2,1)S(1)}, bf16[192,128]{1,0:T(8,128)(2,1)S(1)}, u32[]{:S(2)}, u32[]{:S(2)}) collective-permute-start(bf16[192,128]{1,0:T(8,128)(2,1)S(1)} %collective-permute-done.4), channel_id=1, source_target_pairs={{4,0},{8,4},{12,8},{16,12},{20,16},{24,20},{28,24},{0,28},{5,1},{9... | collective-permute-start | bytes 147464 | tf_op jit(solution)/shard_map/ppermute | solution.py:71
  58.3 6.8 %collective-permute-start.3 = (bf16[192,128]{1,0:T(8,128)(2,1)S(1)}, bf16[192,128]{1,0:T(8,128)(2,1)S(1)}, u32[]{:S(2)}, u32[]{:S(2)}) collective-permute-start(bf16[192,128]{1,0:T(8,128)(2,1)S(1)} %collective-permute-done.2), channel_id=1, source_target_pairs={{0,4},{4,8},{8,12},{12,16},{16,20},{20,24},{24,28},{28,0},{1,5},{5... | collective-permute-start | bytes 147464 | tf_op jit(solution)/shard_map/ppermute | solution.py:69
  58.4 7.6 %collective-permute-start.6 = (bf16[192,128]{1,0:T(8,128)(2,1)S(1)}, bf16[192,128]{1,0:T(8,128)(2,1)S(1)}, u32[]{:S(2)}, u32[]{:S(2)}) collective-permute-start(bf16[192,128]{1,0:T(8,128)(2,1)S(1)} %collective-permute-done.5), channel_id=1, source_target_pairs={{4,0},{8,4},{12,8},{16,12},{20,16},{24,20},{28,24},{0,28},{5,1},{9... | collective-permute-start | bytes 147464 | tf_op jit(solution)/shard_map/ppermute | solution.py:71
Sparse Core Ops, SparseCore 0:
  94.0 23.8 reduce-scatter.1
